TPU v7x, 32 devices: a whole 2x2x4 slice. The times are simulated.
32 devices in a mesh: groups: 2 (over y), tap: 4 (over z), tm: 2 (over x), lag: 2 (over core).
Axes of the slice: x: 2, y: 2, z: 4, core: 2. Of those that a mesh axis runs over, the one named last changes fastest.
Arguments:
- raw_strain: bfloat16 [2048, 1024], P(('groups', 'tap'), 'tm'), parts along dimension 0, may hold values from -4000 to 4000
- spatial_filter: float32 [33], replicated, may hold values from -0.35 to 0.35
- temporal_filter: float32 [255], replicated, may hold values from -0.125 to 0.125
- dest_blocks: int32 [16, 2], P('groups'), parts along dimension 0, may hold values from 0 to 7, as said below
- partner_codes: int32 [16, 128, 64], P(('groups', 'tap', 'lag'), 'tm'), parts along dimension 0, may hold values from 0 to 255, as said below
Outputs:
- coherence: bfloat16 [16, 128, 64, 512], P(('groups', 'tap', 'lag'), 'tm'), parts along dimension 0
There are 2 independent parts, one for each index of `groups`. A program takes and returns all parts, laid end to end along the dimension named above; an argument that names none is the same for every part. Nothing has to cross between parts.
Inputs may be any that keep to these rules, and one draw needn't show every extreme that they name: With n the number of devices along lag, the values dest_blocks[s, j] // n of one row s are distinct and all differ from s // n. `partner_codes`: the 64 codes of one source tap are distinct. Within every source block, each destination slot 0 .. 1 is named by the codes of some tap of that block.
All inputs are finite; a program needn't handle non-finite values.
Results may differ from a plain program's by a relative error of at most 0.022.
Values may be sent and summed in bfloat16 or wider, within the bound.
No kernel may reach another device: no remote copies, remote signals or barrier semaphores. Data moves between devices by JAX's collectives and lax.ppermute only.
A program may use at most 128 MiB of HBM per device.

v0:
```python
import math
import jax
import jax.numpy as jnp
from jax import lax
from jax.sharding import PartitionSpec as P

LAG_COUNT = 512
EPSILON = 1e-06


def extended(cells, sides, width):
    for axis, dim in sides:
        count = lax.axis_size(axis)
        ends = count - 1
        head = lax.slice_in_dim(cells, 0, width, axis=dim)
        tail = lax.slice_in_dim(cells, cells.shape[dim] - width, cells.shape[dim], axis=dim)
        cells = jnp.concatenate(
            [
                lax.ppermute(tail, axis, [(i, (i + 1) % count) for i in range(ends)]),
                cells,
                lax.ppermute(head, axis, [((i + 1) % count, i) for i in range(ends)]),
            ],
            axis=dim,
        )
    return cells


def band_matrix(vector, row_count, col_count):
    length = vector.shape[0]
    padded = jnp.concatenate([vector, jnp.zeros((col_count + 1 - length,), vector.dtype)])
    repeated = jnp.tile(padded, row_count)[: row_count * col_count]
    return repeated.reshape(row_count, col_count)


def split_parts(matrix):
    high_part = matrix.astype(jnp.bfloat16)
    low_part = (matrix - high_part.astype(jnp.float32)).astype(jnp.bfloat16)
    return (high_part, low_part)


def whiten(strain_ext, row_count, spatial_filter, temporal_filter):
    spatial = band_matrix(spatial_filter, row_count, strain_ext.shape[0])
    spatial_high, spatial_low = split_parts(spatial)
    smooth = jnp.einsum("cr,rt->ct", spatial_high, strain_ext, preferred_element_type=jnp.float32)
    smooth = smooth + jnp.einsum(
        "cr,rt->ct", spatial_low, strain_ext, preferred_element_type=jnp.float32
    )
    smooth = smooth.astype(jnp.bfloat16)
    time_half = temporal_filter.shape[0] // 2
    smooth_ext = extended(smooth, (("tm", 1),), time_half)
    temporal = band_matrix(temporal_filter, smooth.shape[1], smooth_ext.shape[1])
    temporal_high, temporal_low = split_parts(temporal)
    whitened = jnp.einsum(
        "cs,ts->ct", smooth_ext, temporal_high, preferred_element_type=jnp.float32
    )
    whitened = whitened + jnp.einsum(
        "cs,ts->ct", smooth_ext, temporal_low, preferred_element_type=jnp.float32
    )
    return whitened.astype(jnp.bfloat16)


def lag_products(buffer, own_row, row_index, lag_count):
    time_total = own_row.shape[0]
    lag_tile = lag_count // 4
    lag_half = lag_count // 2
    picked = jnp.take(buffer, row_index, axis=0)
    padded = jnp.pad(picked, ((0, 0), (lag_half, lag_half)))
    shifted = jnp.concatenate(
        [
            padded[:, shift_step * lag_tile : shift_step * lag_tile + time_total + lag_tile]
            for shift_step in range(4)
        ],
        axis=0,
    )
    toeplitz = band_matrix(own_row, lag_tile, time_total + lag_tile)
    products = lax.dot_general(
        shifted, toeplitz, (((1,), (1,)), ((), ())), preferred_element_type=jnp.float32
    )
    return products.reshape(4, -1, lag_tile).transpose(1, 0, 2).reshape(-1, lag_count)


def per_device(raw_strain, spatial_filter, temporal_filter, dest_blocks, partner_codes):
    taps_here, steps_time = raw_strain.shape
    lag_devices = lax.axis_size("lag")
    tap_devices = lax.axis_size("tap")
    time_devices = lax.axis_size("tm")
    block_taps = taps_here // lag_devices
    lag_index = lax.axis_index("lag")
    tap_index = lax.axis_index("tap")
    spatial_halfwidth = spatial_filter.shape[0] // 2
    strain_ext = extended(raw_strain, (("tap", 0),), spatial_halfwidth)
    whitened = whiten(strain_ext, taps_here, spatial_filter, temporal_filter)
    dest_count = dest_blocks.shape[1]
    by_owner = dest_blocks.reshape(tap_devices, lag_devices, dest_count)
    requests = lax.dynamic_index_in_dim(by_owner, lag_index, 1, keepdims=False)
    req_owner = requests // lag_devices
    req_local = requests % lag_devices
    owner_match = req_owner == tap_index
    local_match = req_local[:, :, None] == jnp.arange(lag_devices, dtype=jnp.int32)[None, None, :]
    selector = jnp.sum(
        jnp.logical_and(owner_match[:, :, None], local_match).astype(jnp.float32), axis=1
    )
    blocks_here = whitened.reshape(lag_devices, block_taps, steps_time)
    outgoing = jnp.einsum(
        "il,lbt->ibt",
        selector.astype(jnp.bfloat16),
        blocks_here,
        preferred_element_type=jnp.float32,
    ).astype(jnp.bfloat16)
    my_blocks = lax.dynamic_index_in_dim(requests, tap_index, 0, keepdims=False)
    my_owners = my_blocks // lag_devices
    code_table = partner_codes[0]
    spread_out = jnp.broadcast_to(
        outgoing[:, None], (tap_devices, time_devices, block_taps, steps_time)
    )
    spread_out = spread_out.reshape(tap_devices * time_devices, block_taps, steps_time)
    arrived = lax.all_to_all(spread_out, ("tap", "tm"), split_axis=0, concat_axis=2, tiled=True)
    arrived = arrived.reshape(block_taps, tap_devices, time_devices * steps_time)
    picked = jnp.take(arrived, my_owners, axis=1)
    buffer = picked.reshape(block_taps * dest_count, -1)
    row_index = code_table % block_taps * dest_count + code_table // block_taps
    own_block = lax.dynamic_slice_in_dim(whitened, lag_index * block_taps, block_taps, 0)
    own_rows = lax.all_to_all(own_block, "tm", split_axis=0, concat_axis=1, tiled=True)
    time_total = own_rows.shape[1]
    energy_own = jnp.sum(jnp.square(own_rows.astype(jnp.float32)), axis=1) / time_total + EPSILON
    energy_buffer = jnp.sum(jnp.square(buffer.astype(jnp.float32)), axis=1) / time_total + EPSILON
    energy_partner = jnp.take(energy_buffer, row_index)
    source_count = own_rows.shape[0]
    partner_count = row_index.shape[1]
    group_size = math.gcd(source_count, 8)
    rows_grouped = own_rows.reshape(source_count // group_size, group_size, time_total)
    index_grouped = row_index.reshape(source_count // group_size, group_size, partner_count)

    def tap_lag_offsets(own_row, indices):
        return lag_products(buffer, own_row, indices, LAG_COUNT)

    def group_products(pieces):
        return jax.vmap(tap_lag_offsets)(pieces[0], pieces[1])

    products = lax.map(group_products, (rows_grouped, index_grouped))
    products = products.reshape(source_count, partner_count, LAG_COUNT)
    norm_scale = jnp.sqrt(energy_own[:, None] * energy_partner) * jnp.sqrt(jnp.float32(time_total))
    coherence = (products / norm_scale[:, :, None]).astype(jnp.bfloat16)
    return coherence[None]


def solution(mesh):
    placed = (
        P(("groups", "tap"), "tm"),
        P(),
        P(),
        P("groups", None),
        P(("groups", "tap", "lag"), "tm", None),
    )
    return jax.shard_map(
        per_device,
        mesh=mesh,
        in_specs=placed,
        out_specs=P(("groups", "tap", "lag"), "tm", None, None),
        check_vma=False,
    )
```

profile of v0, /device:TPU:0, one launch (start us, length us, event | category | flops | bytes accessed | tf_op | source)
XLA Modules:
  0.0 268.1 jit_solution(12425569988358387064)
XLA Ops:
  2.6 6.2 %collective-permute-start = (bf16[16,512]{1,0:T(8,128)(2,1)}, bf16[16,512]{1,0:T(8,128)(2,1)}, u32[]{:S(2)}, u32[]{:S(2)}) collective-permute-start(bf16[16,512]{1,0:T(8,128)(2,1)} %get-tuple-element.88), channel_id=1, source_target_pairs={{0,4},{4,8},{8,12},{1,5},{5,9},{9,13},{2,6},{6,10},{10,14},{3,7},{... | collective-permute-start | bytes 49160 | tf_op jit(solution)/shard_map/ppermute | solution.py:19
  19.7 3.9 %collective-permute-start.2 = (bf16[256,127]{1,0:T(8,128)(2,1)S(1)}, bf16[256,127]{1,0:T(8,128)(2,1)S(1)}, u32[]{:S(2)}, u32[]{:S(2)}) collective-permute-start(bf16[256,127]{1,0:T(8,128)(2,1)S(1)} %get-tuple-element.85), channel_id=1, source_target_pairs={{0,2},{1,3},{4,6},{5,7},{8,10},{9,11},{12,14},{13,15},{16,18},{17,... | collective-permute-start | bytes 195080 | tf_op jit(solution)/shard_map/ppermute | solution.py:19
  25.4 4.3 %collective-permute-done.3 = bf16[256,127]{1,0:T(8,128)(2,1)S(1)} collective-permute-done((bf16[256,127]{1,0:T(8,128)(2,1)S(1)}, bf16[256,127]{1,0:T(8,128)(2,1)S(1)}, u32[]{:S(2)}, u32[]{:S(2)}) %collective-permute-start.3) | collective-permute-done | bytes 65056 | tf_op jit(solution)/shard_map/ppermute | solution.py:21
  40.2 3.8 %all-to-all-start = ((bf16[8,128,512]{1,2,0:T(8,128)(2,1)}), bf16[8,128,512]{1,2,0:T(8,128)(2,1)S(1)}, u32[]{:S(2)}, u32[]{:S(2)}) async-start(bf16[8,128,512]{1,2,0:T(8,128)(2,1)} %bitcast.9), calls=%async_computation | async-start | bytes 2097152 | tf_op jit(solution)/shard_map/all_to_all | solution.py:117
  45.0 21.9 %all-to-all-done = bf16[8,128,512]{1,2,0:T(8,128)(2,1)S(1)} async-done(((bf16[8,128,512]{1,2,0:T(8,128)(2,1)}), bf16[8,128,512]{1,2,0:T(8,128)(2,1)S(1)}, u32[]{:S(2)}, u32[]{:S(2)}) %all-to-all-start) | async-done | bytes 1048608 | tf_op jit(solution)/shard_map/all_to_all | solution.py:117
  68.6 25.7 %gather_fusion.2 = f32[4096]{0:T(1024)S(1)} fusion(f32[256]{0:T(256)S(1)} %add.219, s32[4096]{0:T(1024)S(1)} %broadcast_clamp_fusion), kind=kCustom, calls=%fused_computation.2 | custom fusion | bytes 49152 | tf_op jit(solution)/shard_map/jit(_take)/gather | solution.py:127
  95.3 167.5 %while.12 = (s32[]{:T(128)}, f32[8,8,64,512]{3,2,1,0:T(8,128)}, s32[8,8,64]{2,1,0:T(8,128)S(1)}, bf16[256,1024]{1,0:T(8,128)(2,1)S(1)}, bf16[8,8,1024]{2,1,0:T(8,128)(2,1)S(1)}, /*index=5*/s32[]{:T(128)}, bf16[]{:T(256)}) while((s32[]{:T(128)}, f32[8,8,64,512]{3,2,1,0:T(8,128)}, s32[8,8,64]{2,1,0:T(8,128)S(1)}, ...), condition=%wide.region_2.3_spmd, body=%wide.region_1.2_spmd.sunk | while | flops 623384064 | bytes 57009364 | solution.py:140
  99.1 5.2 %reshape.464 = bf16[1180672]{0:T(1024)(128)(2,1)} reshape(bf16[8,128,1153]{2,1,0:T(8,128)(2,1)S(1)} %tile.36) | data formatting | bytes 4722688 | tf_op jit(solution)/shard_map/while
  104.3 4.2 %tile.37 = bf16[8,147584]{1,0:T(8,128)(2,1)S(1)} reshape(bf16[1180672]{0:T(1024)(128)(2,1)} %reshape.464) | data formatting | bytes 4722688 | tf_op jit(solution)/shard_map/while/body/eval_jaxpr/vmap()/tile | solution.py:31
  119.9 5.2 %reshape.464 = bf16[1180672]{0:T(1024)(128)(2,1)} reshape(bf16[8,128,1153]{2,1,0:T(8,128)(2,1)S(1)} %tile.36) | data formatting | bytes 4722688 | tf_op jit(solution)/shard_map/while
  125.2 4.2 %tile.37 = bf16[8,147584]{1,0:T(8,128)(2,1)S(1)} reshape(bf16[1180672]{0:T(1024)(128)(2,1)} %reshape.464) | data formatting | bytes 4722688 | tf_op jit(solution)/shard_map/while/body/eval_jaxpr/vmap()/tile | solution.py:31
  140.9 5.2 %reshape.464 = bf16[1180672]{0:T(1024)(128)(2,1)} reshape(bf16[8,128,1153]{2,1,0:T(8,128)(2,1)S(1)} %tile.36) | data formatting | bytes 4722688 | tf_op jit(solution)/shard_map/while
  146.1 4.2 %tile.37 = bf16[8,147584]{1,0:T(8,128)(2,1)S(1)} reshape(bf16[1180672]{0:T(1024)(128)(2,1)} %reshape.464) | data formatting | bytes 4722688 | tf_op jit(solution)/shard_map/while/body/eval_jaxpr/vmap()/tile | solution.py:31
  161.8 5.2 %reshape.464 = bf16[1180672]{0:T(1024)(128)(2,1)} reshape(bf16[8,128,1153]{2,1,0:T(8,128)(2,1)S(1)} %tile.36) | data formatting | bytes 4722688 | tf_op jit(solution)/shard_map/while
  167.0 4.2 %tile.37 = bf16[8,147584]{1,0:T(8,128)(2,1)S(1)} reshape(bf16[1180672]{0:T(1024)(128)(2,1)} %reshape.464) | data formatting | bytes 4722688 | tf_op jit(solution)/shard_map/while/body/eval_jaxpr/vmap()/tile | solution.py:31
  182.7 5.2 %reshape.464 = bf16[1180672]{0:T(1024)(128)(2,1)} reshape(bf16[8,128,1153]{2,1,0:T(8,128)(2,1)S(1)} %tile.36) | data formatting | bytes 4722688 | tf_op jit(solution)/shard_map/while
  187.9 4.2 %tile.37 = bf16[8,147584]{1,0:T(8,128)(2,1)S(1)} reshape(bf16[1180672]{0:T(1024)(128)(2,1)} %reshape.464) | data formatting | bytes 4722688 | tf_op jit(solution)/shard_map/while/body/eval_jaxpr/vmap()/tile | solution.py:31
  203.6 5.2 %reshape.464 = bf16[1180672]{0:T(1024)(128)(2,1)} reshape(bf16[8,128,1153]{2,1,0:T(8,128)(2,1)S(1)} %tile.36) | data formatting | bytes 4722688 | tf_op jit(solution)/shard_map/while
  208.8 4.2 %tile.37 = bf16[8,147584]{1,0:T(8,128)(2,1)S(1)} reshape(bf16[1180672]{0:T(1024)(128)(2,1)} %reshape.464) | data formatting | bytes 4722688 | tf_op jit(solution)/shard_map/while/body/eval_jaxpr/vmap()/tile | solution.py:31
  224.5 5.2 %reshape.464 = bf16[1180672]{0:T(1024)(128)(2,1)} reshape(bf16[8,128,1153]{2,1,0:T(8,128)(2,1)S(1)} %tile.36) | data formatting | bytes 4722688 | tf_op jit(solution)/shard_map/while
  229.7 4.2 %tile.37 = bf16[8,147584]{1,0:T(8,128)(2,1)S(1)} reshape(bf16[1180672]{0:T(1024)(128)(2,1)} %reshape.464) | data formatting | bytes 4722688 | tf_op jit(solution)/shard_map/while/body/eval_jaxpr/vmap()/tile | solution.py:31
  245.4 5.2 %reshape.464 = bf16[1180672]{0:T(1024)(128)(2,1)} reshape(bf16[8,128,1153]{2,1,0:T(8,128)(2,1)S(1)} %tile.36) | data formatting | bytes 4722688 | tf_op jit(solution)/shard_map/while
  250.7 4.2 %tile.37 = bf16[8,147584]{1,0:T(8,128)(2,1)S(1)} reshape(bf16[1180672]{0:T(1024)(128)(2,1)} %reshape.464) | data formatting | bytes 4722688 | tf_op jit(solution)/shard_map/while/body/eval_jaxpr/vmap()/tile | solution.py:31
  262.9 5.2 %fusion.11 = bf16[1,64,64,512]{3,2,1,0:T(8,128)(2,1)} fusion(f32[64,64]{1,0:T(8,128)S(1)} %sqrt_multiply_fusion, f32[1,64,64,512]{3,2,1,0:T(8,128)} %bitcast.135), kind=kLoop, calls=%fused_computation.26 | loop fusion | flops 4194304 | bytes 12599296 | tf_op jit(solution)/shard_map/convert_element_type | solution.py:143
  (225 shorter events, 120.5 us)
Async XLA Ops:
  1.3 16.9 %collective-permute-start.1 = (bf16[16,512]{1,0:T(8,128)(2,1)}, bf16[16,512]{1,0:T(8,128)(2,1)}, u32[]{:S(2)}, u32[]{:S(2)}) collective-permute-start(bf16[16,512]{1,0:T(8,128)(2,1)} %get-tuple-element.87), channel_id=1, source_target_pairs={{4,0},{8,4},{12,8},{5,1},{9,5},{13,9},{6,2},{10,6},{14,10},{7,3},{... | collective-permute-start | bytes 49160 | tf_op jit(solution)/shard_map/ppermute | solution.py:21
  2.6 14.9 %collective-permute-start = (bf16[16,512]{1,0:T(8,128)(2,1)}, bf16[16,512]{1,0:T(8,128)(2,1)}, u32[]{:S(2)}, u32[]{:S(2)}) collective-permute-start(bf16[16,512]{1,0:T(8,128)(2,1)} %get-tuple-element.88), channel_id=1, source_target_pairs={{0,4},{4,8},{8,12},{1,5},{5,9},{9,13},{2,6},{6,10},{10,14},{3,7},{... | collective-permute-start | bytes 49160 | tf_op jit(solution)/shard_map/ppermute | solution.py:19
  14.4 3.9 %copy-start.2 = (bf16[256,512]{1,0:T(8,128)(2,1)S(1)}, bf16[256,512]{1,0:T(8,128)(2,1)}, u32[]{:S(2)}) copy-start(bf16[256,512]{1,0:T(8,128)(2,1)} %param.7) | copy-start | bytes 786436
  19.7 5.7 %collective-permute-start.2 = (bf16[256,127]{1,0:T(8,128)(2,1)S(1)}, bf16[256,127]{1,0:T(8,128)(2,1)S(1)}, u32[]{:S(2)}, u32[]{:S(2)}) collective-permute-start(bf16[256,127]{1,0:T(8,128)(2,1)S(1)} %get-tuple-element.85), channel_id=1, source_target_pairs={{0,2},{1,3},{4,6},{5,7},{8,10},{9,11},{12,14},{13,15},{16,18},{17,... | collective-permute-start | bytes 195080 | tf_op jit(solution)/shard_map/ppermute | solution.py:19
  23.6 6.2 %collective-permute-start.3 = (bf16[256,127]{1,0:T(8,128)(2,1)S(1)}, bf16[256,127]{1,0:T(8,128)(2,1)S(1)}, u32[]{:S(2)}, u32[]{:S(2)}) collective-permute-start(bf16[256,127]{1,0:T(8,128)(2,1)S(1)} %get-tuple-element.86), channel_id=1, source_target_pairs={{2,0},{3,1},{6,4},{7,5},{10,8},{11,9},{14,12},{15,13},{18,16},{19,... | collective-permute-start | bytes 195080 | tf_op jit(solution)/shard_map/ppermute | solution.py:21
  31.2 7.8 %all-to-all-start.1 = ((bf16[2,64,512]{2,1,0:T(8,128)(2,1)}), bf16[2,64,512]{2,1,0:T(8,128)(2,1)S(1)}, u32[]{:S(2)}, u32[]{:S(2)}) async-start(bf16[2,64,512]{2,1,0:T(8,128)(2,1)} %bitcast.15), calls=%async_computation.1 | async-start | bytes 262144 | tf_op jit(solution)/shard_map/all_to_all | solution.py:123
  35.1 9.3 %copy-start.3 = (s32[1,64,64]{2,1,0:T(8,128)S(1)}, s32[1,64,64]{2,1,0:T(8,128)}, u32[]{:S(2)}) copy-start(s32[1,64,64]{2,1,0:T(8,128)} %param.11) | copy-start | bytes 49156
  40.2 26.7 %all-to-all-start = ((bf16[8,128,512]{1,2,0:T(8,128)(2,1)}), bf16[8,128,512]{1,2,0:T(8,128)(2,1)S(1)}, u32[]{:S(2)}, u32[]{:S(2)}) async-start(bf16[8,128,512]{1,2,0:T(8,128)(2,1)} %bitcast.9), calls=%async_computation | async-start | bytes 2097152 | tf_op jit(solution)/shard_map/all_to_all | solution.py:117
  108.5 2.0 copy-start.1
  110.5 1.7 slice-start
  129.4 2.0 copy-start.1
  131.4 1.7 slice-start
  150.3 2.0 copy-start.1
  152.4 1.7 slice-start
  171.3 2.0 copy-start.1
  173.3 1.7 slice-start
  192.2 2.0 copy-start.1
  194.2 1.7 slice-start
  213.1 2.0 copy-start.1
  215.1 1.7 slice-start
  234.0 2.0 copy-start.1
  236.0 1.7 slice-start
  254.9 2.0 copy-start.1
  256.9 1.7 slice-start
  (8 other events, 11.3 us)
where the time goes:
time: 270 us; the launch traced here: 268 us
  local copies, waits for them, and re-layouts  183 us (68%)
  waiting for transfers between devices  30.3 us (11%)
  starting transfers between devices  19.8 us (7%)
  matrix products  17.7 us (7%)
  other arithmetic  15.9 us (6%)
    while x40, local copies, waits for them, and re-layouts  57.8 us
    another operation x20, local copies, waits for them, and re-layouts, band_matrix(): repeated = jnp.tile(padded, row_count)[:row_count * col_count]  36.9 us
    gather x2, local copies, waits for them, and re-layouts, per_device(): energy_partner = jnp.take(energy_buffer, row_index)  25.8 us
    all_to_all x1, waiting for transfers between devices, per_device(): lax.all_to_all(spread_out, ('tap', 'tm'), split_axis=0, concat_axis=2, ti...  21.9 us
    gather x8, local copies, waits for them, and re-layouts, lag_products(): picked = jnp.take(buffer, row_index, axis=0)  16.5 us
    dot_general x8, matrix products, lag_products(): lax.dot_general(shifted, toeplitz, (((1,), (1,)), ((), ())), preferred_el...  15.8 us
    ppermute x2, starting transfers between devices, extended(): lax.ppermute(tail, axis, [(i, (i + 1) % count) for i in range(ends)])  10 us
    select_n x16, other arithmetic, lag_products(): picked = jnp.take(buffer, row_index, axis=0)  9.78 us
  transfers between devices with their start and end apart: 6, of which 4 were waited for; matrix products, arithmetic and copies ran while one was open for 4% of the time, Pallas kernels for 0%

commit v1 on v0

--- a/solution.py
+++ b/solution.py
@@ -120,7 +120,14 @@
     buffer = picked.reshape(block_taps * dest_count, -1)
     row_index = code_table % block_taps * dest_count + code_table // block_taps
     own_block = lax.dynamic_slice_in_dim(whitened, lag_index * block_taps, block_taps, 0)
-    own_rows = lax.all_to_all(own_block, "tm", split_axis=0, concat_axis=1, tiled=True)
+
+    def search_flows(u_in):
+        return jnp.concatenate(
+            lax.all_to_all(jnp.stack(jnp.split(u_in, lax.axis_size("tm"), 0), axis=0), "tm", 0, 0),
+            1,
+        )
+
+    own_rows = search_flows(own_block)
     time_total = own_rows.shape[1]
     energy_own = jnp.sum(jnp.square(own_rows.astype(jnp.float32)), axis=1) / time_total + EPSILON
     energy_buffer = jnp.sum(jnp.square(buffer.astype(jnp.float32)), axis=1) / time_total + EPSILON

time: 270 us -> 269 us (level)
  no operation moved by 1% of the time
where the time goes in v1:
time: 269 us; the launch traced here: 268 us
  local copies, waits for them, and re-layouts  183 us (68%)
  waiting for transfers between devices  30.3 us (11%)
  starting transfers between devices  19.8 us (7%)
  matrix products  17.7 us (7%)
  other arithmetic  16.5 us (6%)
    while x40, local copies, waits for them, and re-layouts  57.8 us
    another operation x20, local copies, waits for them, and re-layouts, band_matrix(): repeated = jnp.tile(padded, row_count)[:row_count * col_count]  36.9 us
    gather x2, local copies, waits for them, and re-layouts, per_device(): energy_partner = jnp.take(energy_buffer, row_index)  25.8 us
    all_to_all x1, waiting for transfers between devices, per_device(): lax.all_to_all(spread_out, ('tap', 'tm'), split_axis=0, concat_axis=2, ti...  21.9 us
    gather x8, local copies, waits for them, and re-layouts, lag_products(): picked = jnp.take(buffer, row_index, axis=0)  16.5 us
    dot_general x8, matrix products, lag_products(): lax.dot_general(shifted, toeplitz, (((1,), (1,)), ((), ())), preferred_el...  15.8 us
    ppermute x2, starting transfers between devices, extended(): lax.ppermute(tail, axis, [(i, (i + 1) % count) for i in range(ends)])  9.98 us
    select_n x16, other arithmetic, lag_products(): picked = jnp.take(buffer, row_index, axis=0)  9.71 us
  transfers between devices with their start and end apart: 6, of which 4 were waited for; matrix products, arithmetic and copies ran while one was open for 4% of the time, Pallas kernels for 0%

profile of v1, /device:TPU:0, one launch (start us, length us, event | category | flops | bytes accessed | tf_op | source)
XLA Modules:
  0.0 268.0 jit_solution(11840539511501396997)
XLA Ops:
  2.6 6.2 %collective-permute-start = (bf16[16,512]{1,0:T(8,128)(2,1)}, bf16[16,512]{1,0:T(8,128)(2,1)}, u32[]{:S(2)}, u32[]{:S(2)}) collective-permute-start(bf16[16,512]{1,0:T(8,128)(2,1)} %get-tuple-element.90), channel_id=1, source_target_pairs={{0,4},{4,8},{8,12},{1,5},{5,9},{9,13},{2,6},{6,10},{10,14},{3,7},{... | collective-permute-start | bytes 49160 | tf_op jit(solution)/shard_map/ppermute | solution.py:19
  19.7 3.8 %collective-permute-start.2 = (bf16[256,127]{1,0:T(8,128)(2,1)S(1)}, bf16[256,127]{1,0:T(8,128)(2,1)S(1)}, u32[]{:S(2)}, u32[]{:S(2)}) collective-permute-start(bf16[256,127]{1,0:T(8,128)(2,1)S(1)} %get-tuple-element.87), channel_id=1, source_target_pairs={{0,2},{1,3},{4,6},{5,7},{8,10},{9,11},{12,14},{13,15},{16,18},{17,... | collective-permute-start | bytes 195080 | tf_op jit(solution)/shard_map/ppermute | solution.py:19
  25.4 4.3 %collective-permute-done.3 = bf16[256,127]{1,0:T(8,128)(2,1)S(1)} collective-permute-done((bf16[256,127]{1,0:T(8,128)(2,1)S(1)}, bf16[256,127]{1,0:T(8,128)(2,1)S(1)}, u32[]{:S(2)}, u32[]{:S(2)}) %collective-permute-start.3) | collective-permute-done | bytes 65056 | tf_op jit(solution)/shard_map/ppermute | solution.py:21
  40.2 3.9 %all-to-all-start = ((bf16[8,128,512]{1,2,0:T(8,128)(2,1)}), bf16[8,128,512]{1,2,0:T(8,128)(2,1)S(1)}, u32[]{:S(2)}, u32[]{:S(2)}) async-start(bf16[8,128,512]{1,2,0:T(8,128)(2,1)} %bitcast.9), calls=%async_computation | async-start | bytes 2097152 | tf_op jit(solution)/shard_map/all_to_all | solution.py:117
  45.0 21.9 %all-to-all-done = bf16[8,128,512]{1,2,0:T(8,128)(2,1)S(1)} async-done(((bf16[8,128,512]{1,2,0:T(8,128)(2,1)}), bf16[8,128,512]{1,2,0:T(8,128)(2,1)S(1)}, u32[]{:S(2)}, u32[]{:S(2)}) %all-to-all-start) | async-done | bytes 1048608 | tf_op jit(solution)/shard_map/all_to_all | solution.py:117
  68.6 25.7 %gather_fusion.2 = f32[4096]{0:T(1024)S(1)} fusion(f32[256]{0:T(256)S(1)} %add.219, s32[4096]{0:T(1024)S(1)} %broadcast_clamp_fusion), kind=kCustom, calls=%fused_computation.2 | custom fusion | bytes 49152 | tf_op jit(solution)/shard_map/jit(_take)/gather | solution.py:134
  95.3 167.4 %while.12 = (s32[]{:T(128)}, f32[8,8,64,512]{3,2,1,0:T(8,128)}, s32[8,8,64]{2,1,0:T(8,128)S(1)}, bf16[256,1024]{1,0:T(8,128)(2,1)S(1)}, bf16[8,8,1024]{2,1,0:T(8,128)(2,1)S(1)}, /*index=5*/s32[]{:T(128)}, bf16[]{:T(256)}) while((s32[]{:T(128)}, f32[8,8,64,512]{3,2,1,0:T(8,128)}, s32[8,8,64]{2,1,0:T(8,128)S(1)}, ...), condition=%wide.region_2.3_spmd, body=%wide.region_1.2_spmd.sunk | while | flops 623384064 | bytes 57009364 | solution.py:147
  99.1 5.2 %reshape.461 = bf16[1180672]{0:T(1024)(128)(2,1)} reshape(bf16[8,128,1153]{2,1,0:T(8,128)(2,1)S(1)} %tile.36) | data formatting | bytes 4722688 | tf_op jit(solution)/shard_map/while
  104.3 4.2 %tile.37 = bf16[8,147584]{1,0:T(8,128)(2,1)S(1)} reshape(bf16[1180672]{0:T(1024)(128)(2,1)} %reshape.461) | data formatting | bytes 4722688 | tf_op jit(solution)/shard_map/while/body/eval_jaxpr/vmap()/tile | solution.py:31
  119.9 5.2 %reshape.461 = bf16[1180672]{0:T(1024)(128)(2,1)} reshape(bf16[8,128,1153]{2,1,0:T(8,128)(2,1)S(1)} %tile.36) | data formatting | bytes 4722688 | tf_op jit(solution)/shard_map/while
  125.2 4.2 %tile.37 = bf16[8,147584]{1,0:T(8,128)(2,1)S(1)} reshape(bf16[1180672]{0:T(1024)(128)(2,1)} %reshape.461) | data formatting | bytes 4722688 | tf_op jit(solution)/shard_map/while/body/eval_jaxpr/vmap()/tile | solution.py:31
  140.9 5.2 %reshape.461 = bf16[1180672]{0:T(1024)(128)(2,1)} reshape(bf16[8,128,1153]{2,1,0:T(8,128)(2,1)S(1)} %tile.36) | data formatting | bytes 4722688 | tf_op jit(solution)/shard_map/while
  146.1 4.2 %tile.37 = bf16[8,147584]{1,0:T(8,128)(2,1)S(1)} reshape(bf16[1180672]{0:T(1024)(128)(2,1)} %reshape.461) | data formatting | bytes 4722688 | tf_op jit(solution)/shard_map/while/body/eval_jaxpr/vmap()/tile | solution.py:31
  161.8 5.2 %reshape.461 = bf16[1180672]{0:T(1024)(128)(2,1)} reshape(bf16[8,128,1153]{2,1,0:T(8,128)(2,1)S(1)} %tile.36) | data formatting | bytes 4722688 | tf_op jit(solution)/shard_map/while
  167.0 4.2 %tile.37 = bf16[8,147584]{1,0:T(8,128)(2,1)S(1)} reshape(bf16[1180672]{0:T(1024)(128)(2,1)} %reshape.461) | data formatting | bytes 4722688 | tf_op jit(solution)/shard_map/while/body/eval_jaxpr/vmap()/tile | solution.py:31
  182.7 5.2 %reshape.461 = bf16[1180672]{0:T(1024)(128)(2,1)} reshape(bf16[8,128,1153]{2,1,0:T(8,128)(2,1)S(1)} %tile.36) | data formatting | bytes 4722688 | tf_op jit(solution)/shard_map/while
  187.9 4.2 %tile.37 = bf16[8,147584]{1,0:T(8,128)(2,1)S(1)} reshape(bf16[1180672]{0:T(1024)(128)(2,1)} %reshape.461) | data formatting | bytes 4722688 | tf_op jit(solution)/shard_map/while/body/eval_jaxpr/vmap()/tile | solution.py:31
  203.6 5.2 %reshape.461 = bf16[1180672]{0:T(1024)(128)(2,1)} reshape(bf16[8,128,1153]{2,1,0:T(8,128)(2,1)S(1)} %tile.36) | data formatting | bytes 4722688 | tf_op jit(solution)/shard_map/while
  208.8 4.2 %tile.37 = bf16[8,147584]{1,0:T(8,128)(2,1)S(1)} reshape(bf16[1180672]{0:T(1024)(128)(2,1)} %reshape.461) | data formatting | bytes 4722688 | tf_op jit(solution)/shard_map/while/body/eval_jaxpr/vmap()/tile | solution.py:31
  224.5 5.2 %reshape.461 = bf16[1180672]{0:T(1024)(128)(2,1)} reshape(bf16[8,128,1153]{2,1,0:T(8,128)(2,1)S(1)} %tile.36) | data formatting | bytes 4722688 | tf_op jit(solution)/shard_map/while
  229.7 4.2 %tile.37 = bf16[8,147584]{1,0:T(8,128)(2,1)S(1)} reshape(bf16[1180672]{0:T(1024)(128)(2,1)} %reshape.461) | data formatting | bytes 4722688 | tf_op jit(solution)/shard_map/while/body/eval_jaxpr/vmap()/tile | solution.py:31
  245.4 5.2 %reshape.461 = bf16[1180672]{0:T(1024)(128)(2,1)} reshape(bf16[8,128,1153]{2,1,0:T(8,128)(2,1)S(1)} %tile.36) | data formatting | bytes 4722688 | tf_op jit(solution)/shard_map/while
  250.6 4.2 %tile.37 = bf16[8,147584]{1,0:T(8,128)(2,1)S(1)} reshape(bf16[1180672]{0:T(1024)(128)(2,1)} %reshape.461) | data formatting | bytes 4722688 | tf_op jit(solution)/shard_map/while/body/eval_jaxpr/vmap()/tile | solution.py:31
  262.8 5.2 %fusion.11 = bf16[1,64,64,512]{3,2,1,0:T(8,128)(2,1)} fusion(f32[64,64]{1,0:T(8,128)S(1)} %sqrt_multiply_fusion, f32[1,64,64,512]{3,2,1,0:T(8,128)} %bitcast.138), kind=kLoop, calls=%fused_computation.26 | loop fusion | flops 4194304 | bytes 12599296 | tf_op jit(solution)/shard_map/convert_element_type | solution.py:150
  (226 shorter events, 120.4 us)
Async XLA Ops:
  1.3 16.9 %collective-permute-start.1 = (bf16[16,512]{1,0:T(8,128)(2,1)}, bf16[16,512]{1,0:T(8,128)(2,1)}, u32[]{:S(2)}, u32[]{:S(2)}) collective-permute-start(bf16[16,512]{1,0:T(8,128)(2,1)} %get-tuple-element.89), channel_id=1, source_target_pairs={{4,0},{8,4},{12,8},{5,1},{9,5},{13,9},{6,2},{10,6},{14,10},{7,3},{... | collective-permute-start | bytes 49160 | tf_op jit(solution)/shard_map/ppermute | solution.py:21
  2.6 14.9 %collective-permute-start = (bf16[16,512]{1,0:T(8,128)(2,1)}, bf16[16,512]{1,0:T(8,128)(2,1)}, u32[]{:S(2)}, u32[]{:S(2)}) collective-permute-start(bf16[16,512]{1,0:T(8,128)(2,1)} %get-tuple-element.90), channel_id=1, source_target_pairs={{0,4},{4,8},{8,12},{1,5},{5,9},{9,13},{2,6},{6,10},{10,14},{3,7},{... | collective-permute-start | bytes 49160 | tf_op jit(solution)/shard_map/ppermute | solution.py:19
  14.4 3.9 %copy-start.2 = (bf16[256,512]{1,0:T(8,128)(2,1)S(1)}, bf16[256,512]{1,0:T(8,128)(2,1)}, u32[]{:S(2)}) copy-start(bf16[256,512]{1,0:T(8,128)(2,1)} %param.7) | copy-start | bytes 786436
  19.7 5.7 %collective-permute-start.2 = (bf16[256,127]{1,0:T(8,128)(2,1)S(1)}, bf16[256,127]{1,0:T(8,128)(2,1)S(1)}, u32[]{:S(2)}, u32[]{:S(2)}) collective-permute-start(bf16[256,127]{1,0:T(8,128)(2,1)S(1)} %get-tuple-element.87), channel_id=1, source_target_pairs={{0,2},{1,3},{4,6},{5,7},{8,10},{9,11},{12,14},{13,15},{16,18},{17,... | collective-permute-start | bytes 195080 | tf_op jit(solution)/shard_map/ppermute | solution.py:19
  23.5 6.2 %collective-permute-start.3 = (bf16[256,127]{1,0:T(8,128)(2,1)S(1)}, bf16[256,127]{1,0:T(8,128)(2,1)S(1)}, u32[]{:S(2)}, u32[]{:S(2)}) collective-permute-start(bf16[256,127]{1,0:T(8,128)(2,1)S(1)} %get-tuple-element.88), channel_id=1, source_target_pairs={{2,0},{3,1},{6,4},{7,5},{10,8},{11,9},{14,12},{15,13},{18,16},{19,... | collective-permute-start | bytes 195080 | tf_op jit(solution)/shard_map/ppermute | solution.py:21
  31.2 7.8 %all-to-all-start.1 = ((bf16[2,64,512]{2,1,0:T(8,128)(2,1)}), bf16[2,64,512]{2,1,0:T(8,128)(2,1)S(1)}, u32[]{:S(2)}, u32[]{:S(2)}) async-start(bf16[2,64,512]{2,1,0:T(8,128)(2,1)} %pad_maximum_fusion.3), calls=%async_computation.1 | async-start | bytes 262144 | tf_op jit(solution)/shard_map/all_to_all | solution.py:126
  35.1 9.3 %copy-start.3 = (s32[1,64,64]{2,1,0:T(8,128)S(1)}, s32[1,64,64]{2,1,0:T(8,128)}, u32[]{:S(2)}) copy-start(s32[1,64,64]{2,1,0:T(8,128)} %param.11) | copy-start | bytes 49156
  40.2 26.7 %all-to-all-start = ((bf16[8,128,512]{1,2,0:T(8,128)(2,1)}), bf16[8,128,512]{1,2,0:T(8,128)(2,1)S(1)}, u32[]{:S(2)}, u32[]{:S(2)}) async-start(bf16[8,128,512]{1,2,0:T(8,128)(2,1)} %bitcast.9), calls=%async_computation | async-start | bytes 2097152 | tf_op jit(solution)/shard_map/all_to_all | solution.py:117
  108.5 2.0 copy-start.1
  110.5 1.7 slice-start
  129.4 2.0 copy-start.1
  131.4 1.7 slice-start
  150.3 2.0 copy-start.1
  152.3 1.7 slice-start
  171.2 2.0 copy-start.1
  173.2 1.7 slice-start
  192.1 2.0 copy-start.1
  194.1 1.7 slice-start
  213.0 2.0 copy-start.1
  215.0 1.7 slice-start
  233.9 2.0 copy-start.1
  235.9 1.7 slice-start
  254.8 2.0 copy-start.1
  256.9 1.7 slice-start
  (8 other events, 11.3 us)
